TPU v7x, 32 devices: a whole 2x2x4 slice. The times are simulated.
32 devices in a mesh: view: 2 (over core), dom: 16 (over z, y, x).
Axes of the slice: x: 2, y: 2, z: 4, core: 2. Of those that a mesh axis runs over, the one named last changes fastest.
Arguments:
- features: bfloat16 [16384, 512], P('dom'), may hold values from -6 to 6
- feat_keep: int32 [2, 512], P('view'), may hold values 0 or 1
- w_first: bfloat16 [512, 512], replicated, may hold values from -0.25 to 0.25
- w_second: bfloat16 [512, 512], replicated, may hold values from -0.25 to 0.25
- adjacency: bfloat16 [2, 1024, 128, 128], P('view', 'dom'), may hold values from 0 to 0.015625
- tile_src: int32 [2, 128, 8], P('view', 'dom'), may hold values from 0 to 8, as said below
- halo_rows: int32 [16, 16, 8], P('dom'), may hold values from 0 to 1023
- halo_live: int32 [16, 16], P('dom'), may hold values from 0 to 8, as said below
- neg_pick: int32 [16, 16, 8], P('dom'), may hold values from 0 to 1023
Outputs:
- node_loss: float32 [2, 16384], P('view', 'dom')
- grad_first: float32 [512, 512], replicated
- grad_second: float32 [512, 512], replicated
Inputs may be any that keep to these rules, and one draw needn't show every extreme that they name: `tile_src`: the last tile of the first block of every partition reads its last halo block. `halo_live`: some receiver gets 8 live rows from every sender.
All inputs are finite; a program needn't handle non-finite values. No bound on the sum of `feat_keep` on one device may be relied on, other than what follows from the above.
Results may differ from a plain program's by a relative error of at most 0.0015.
The roundings to bfloat16 on the way count: a program that leaves them out, or rounds other values in their place, can miss the bound.
Values may be sent and summed in bfloat16 or wider, within the bound.
No kernel may reach another device: no remote copies, remote signals or barrier semaphores. Data moves between devices by JAX's collectives and lax.ppermute only.
A program may use at most 128 MiB of HBM per device.

v0:
```python
import jax
import jax.numpy as jnp
from jax import lax
from jax.sharding import PartitionSpec as P

inv_temp = 5.0
norm_eps = 1e-06


def swapped(array, axis, distance):
    return lax.ppermute(array, axis, [(i, i ^ 1 << distance) for i in range(lax.axis_size(axis))])


def mix_blocks(ext_blocks, tiles, sources, inv_deg):
    picked = ext_blocks[sources]
    summed = jnp.einsum("ntij,ntjw->niw", tiles, picked, preferred_element_type=jnp.float32)
    own_rows = ext_blocks[: sources.shape[0]].astype(jnp.float32)
    return ((own_rows + summed) * inv_deg[:, :, None]).astype(jnp.bfloat16)


def spread_back(grad_mixed, tiles, sources, inv_deg, total_blocks):
    scaled = (grad_mixed * inv_deg[:, :, None]).astype(jnp.bfloat16)
    spread = jnp.einsum("ntij,niw->ntjw", tiles, scaled, preferred_element_type=jnp.float32)
    ext_grad = jnp.zeros((total_blocks, grad_mixed.shape[1], grad_mixed.shape[2]), jnp.float32)
    ext_grad = ext_grad.at[sources].add(spread)
    return ext_grad.at[: sources.shape[0]].add(scaled.astype(jnp.float32))


def contrast(unit, partner, negatives):
    unit_f = unit.astype(jnp.float32)
    partner_f = partner.astype(jnp.float32)
    positive = inv_temp * jnp.sum(unit_f * partner_f, axis=1)
    scores = inv_temp * jnp.dot(unit, negatives.T, preferred_element_type=jnp.float32)
    expo = jnp.exp(scores)
    total = jnp.exp(positive) + jnp.sum(expo, axis=1)
    node_loss = jnp.log(total) - positive
    prob = (expo / total[:, None]).astype(jnp.bfloat16)
    own_share = jnp.exp(positive) / total
    share_less = own_share - 1.0
    g_anchor = inv_temp * (
        share_less[:, None] * partner_f
        + jnp.dot(prob, negatives, preferred_element_type=jnp.float32)
    )
    g_partner = inv_temp * share_less[:, None] * unit_f
    g_neg = inv_temp * jnp.dot(prob.T, unit, preferred_element_type=jnp.float32)
    return (node_loss, g_anchor, g_partner, g_neg, share_less)


def per_device(
    features, feat_keep, w_first, w_second, adjacency, tile_src, halo_rows, halo_live, neg_pick
):
    row_count, feat_width = features.shape
    hid_width = w_first.shape[1]
    block_rows = adjacency.shape[2]
    block_count = tile_src.shape[1]
    tile_count = tile_src.shape[2]
    part_count = lax.axis_size("dom")
    slot_cap = halo_rows.shape[2]
    neg_count = neg_pick.shape[2]
    tiles = adjacency[0].reshape(block_count, tile_count, block_rows, block_rows)
    sources = tile_src[0]
    inv_deg = 1.0 / (1.0 + jnp.sum(tiles.astype(jnp.float32), axis=(1, 3)))
    keep_cols = feat_keep[0].astype(jnp.bfloat16)
    send_rows = halo_rows[0]
    live_slots = lax.broadcasted_iota(jnp.int32, (part_count, slot_cap), 1) < halo_live[0][:, None]
    live_bf = live_slots.astype(jnp.bfloat16)[:, :, None]
    masked = features * keep_cols
    outgoing = masked[send_rows] * live_bf
    incoming = lax.all_to_all(outgoing, "dom", split_axis=0, concat_axis=0, tiled=True).reshape(
        part_count * slot_cap, feat_width
    )
    ext_first = jnp.concatenate([masked, incoming], 0).reshape(-1, block_rows, feat_width)
    mixed_first = mix_blocks(ext_first, tiles, sources, inv_deg).reshape(row_count, feat_width)
    pre_act = jnp.dot(mixed_first, w_first, preferred_element_type=jnp.float32)
    hidden = jnp.maximum(pre_act, 0.0).astype(jnp.bfloat16)
    hidden_out = hidden[send_rows] * live_bf
    hidden_in = lax.all_to_all(hidden_out, "dom", split_axis=0, concat_axis=0, tiled=True).reshape(
        part_count * slot_cap, hid_width
    )
    ext_second = jnp.concatenate([hidden, hidden_in], 0).reshape(-1, block_rows, hid_width)
    mixed_second = mix_blocks(ext_second, tiles, sources, inv_deg).reshape(row_count, hid_width)
    projected = jnp.dot(mixed_second, w_second, preferred_element_type=jnp.float32)
    inv_norm = lax.rsqrt(jnp.sum(projected * projected, axis=1, keepdims=True) + norm_eps)
    normed = projected * inv_norm
    unit = normed.astype(jnp.bfloat16)
    partner = swapped(unit, "view", 0)
    pick_rows = neg_pick[0].reshape(-1)
    neg_out = partner[neg_pick[0]]
    negatives = lax.all_to_all(neg_out, "dom", split_axis=0, concat_axis=0, tiled=True).reshape(
        part_count * neg_count, hid_width
    )
    node_loss, g_anchor, g_partner, g_neg, share_less = contrast(unit, partner, negatives)
    returned = lax.all_to_all(
        g_neg.reshape(part_count, neg_count, hid_width),
        "dom",
        split_axis=0,
        concat_axis=0,
        tiled=True,
    )
    g_partner = g_partner.at[pick_rows].add(returned.reshape(-1, hid_width))
    g_emb = g_anchor + swapped(g_partner, "view", 0)
    inner = jnp.sum(normed * g_emb, axis=1, keepdims=True)
    g_proj = ((g_emb - normed * inner) * inv_norm).astype(jnp.bfloat16)
    grad_second = jnp.einsum("ih,ik->hk", mixed_second, g_proj, preferred_element_type=jnp.float32)
    g_mixed = jnp.einsum("ik,hk->ih", g_proj, w_second, preferred_element_type=jnp.float32)
    ext_grad = spread_back(
        g_mixed.reshape(block_count, block_rows, hid_width),
        tiles,
        sources,
        inv_deg,
        ext_second.shape[0],
    )
    flat_grad = ext_grad.reshape(-1, hid_width)
    halo_grad = flat_grad[row_count:].reshape(part_count, slot_cap, hid_width)
    back_grad = lax.all_to_all(
        halo_grad.astype(jnp.bfloat16), "dom", split_axis=0, concat_axis=0, tiled=True
    ).astype(halo_grad.dtype)
    back_grad = back_grad * live_slots.astype(jnp.float32)[:, :, None]
    g_hidden = flat_grad[:row_count].at[send_rows.reshape(-1)].add(back_grad.reshape(-1, hid_width))
    g_pre = jnp.where(pre_act > 0, g_hidden, 0.0).astype(jnp.bfloat16)
    grad_first = jnp.einsum("if,ih->fh", mixed_first, g_pre, preferred_element_type=jnp.float32)
    summed = lax.psum((grad_first, grad_second), ("view", "dom"))
    return (node_loss[None, :], summed[0], summed[1])


def solution(mesh):
    placed = (
        P("dom", None),
        P("view", None),
        P(),
        P(),
        P("view", "dom", None, None),
        P("view", "dom", None),
        P("dom", None, None),
        P("dom", None),
        P("dom", None, None),
    )
    return jax.shard_map(
        per_device,
        mesh=mesh,
        in_specs=placed,
        out_specs=(P("view", "dom"), P(), P()),
        check_vma=False,
    )
```

profile of v0, /device:TPU:0, one launch (start us, length us, event | category | flops | bytes accessed | tf_op | source)
XLA Modules:
  0.0 339.7 jit_solution(16240361134284853910)
XLA Ops:
  7.2 0.9 convert_reduce_fusion.1
  8.9 1.3 fusion.26
  10.2 2.3 broadcast_multiply_fusion
  12.5 2.2 gather_fusion
  15.5 8.3 %all-to-all-start = ((bf16[16,8,512]{2,1,0:T(8,128)(2,1)}), bf16[16,8,512]{2,1,0:T(8,128)(2,1)S(1)}, u32[]{:S(2)}, u32[]{:S(2)}) async-start(bf16[16,8,512]{2,1,0:T(8,128)(2,1)} %bitcast_multiply_fusion.1), calls=%async_computation | async-start | bytes 262144 | tf_op jit(solution)/shard_map/all_to_all | solution.py:69
  24.6 7.0 %all-to-all-done = bf16[16,8,512]{2,1,0:T(8,128)(2,1)S(1)} async-done(((bf16[16,8,512]{2,1,0:T(8,128)(2,1)}), bf16[16,8,512]{2,1,0:T(8,128)(2,1)S(1)}, u32[]{:S(2)}, u32[]{:S(2)}) %all-to-all-start) | async-done | bytes 131104 | tf_op jit(solution)/shard_map/all_to_all | solution.py:69
  31.6 1.3 pad_maximum_fusion
  33.0 5.5 %gather_fusion.1 = bf16[64,128,512]{2,1,0:T(8,128)(2,1)} fusion(bf16[9,128,512]{2,1,0:T(8,128)(2,1)S(1)} %bitcast.105, s32[1024]{0:T(1024)S(1)} %pad_clamp_fusion.1), kind=kCustom, calls=%fused_computation.1 | custom fusion | bytes 16777472 | tf_op jit(solution)/shard_map/gather | solution.py:15
  38.5 5.4 %fusion.7 = bf16[8,128,512]{2,1,0:T(8,128)(2,1)S(1)} fusion(bf16[8,128,512]{2,1,0:T(8,128)(2,1)S(1)} %bitcast.114, bf16[8,8,128,128]{3,2,1,0:T(8,128)(2,1)} %bitcast.107, bf16[8,8,128,512]{3,2,1,0:T(8,128)(2,1)} %bitcast.111, f32[8,128]{1,0:T(8,128)S(1)} %add_divide_fusion), kind=kOutput, calls=%fused_computation.23 | convolution fusion | flops 1075838976 | bytes 12587008 | tf_op jit(solution)/shard_map/ntij,ntjw->niw/dot_general | solution.py:16
  43.9 2.1 maximum_convert_fusion
  45.9 0.8 gather_fusion.2
  46.9 10.4 %all_to_all.25 = bf16[16,8,512]{2,1,0:T(8,128)(2,1)S(1)} all-to-all(bf16[16,8,512]{2,1,0:T(8,128)(2,1)S(1)} %bitcast_multiply_fusion), channel_id=1, replica_groups=mesh['view'=2,'dom'=16] {'dom'}, dimensions={0} | all-to-all | bytes 262144 | tf_op jit(solution)/shard_map/all_to_all | solution.py:77
  57.3 5.5 %gather_fusion.3 = bf16[64,128,512]{2,1,0:T(8,128)(2,1)} fusion(bf16[9,128,512]{2,1,0:T(8,128)(2,1)S(1)} %bitcast.104, s32[1024]{0:T(1024)S(1)} %pad_clamp_fusion.1), kind=kCustom, calls=%fused_computation.3 | custom fusion | bytes 16777472 | tf_op jit(solution)/shard_map/gather | solution.py:15
  62.9 5.3 %fusion.5 = bf16[8,128,512]{2,1,0:T(8,128)(2,1)S(1)} fusion(bf16[8,128,512]{2,1,0:T(8,128)(2,1)S(1)} %bitcast.115, bf16[8,8,128,128]{3,2,1,0:T(8,128)(2,1)} %bitcast.108, bf16[8,8,128,512]{3,2,1,0:T(8,128)(2,1)} %bitcast.110, f32[8,128]{1,0:T(8,128)S(1)} %add_divide_fusion), kind=kOutput, calls=%fused_computation.20 | convolution fusion | flops 1075838976 | bytes 12587008 | tf_op jit(solution)/shard_map/ntij,ntjw->niw/dot_general | solution.py:16
  68.2 0.8 multiply_reduce_fusion.1
  69.0 1.2 multiply_convert_fusion.2
  70.4 2.8 collective-permute-done
  73.2 2.3 copy.31
  75.5 2.9 gather_fusion.4
  78.4 3.5 %all-to-all-start.2 = ((bf16[16,8,512]{2,1,0:T(8,128)(2,1)}), bf16[16,8,512]{2,1,0:T(8,128)(2,1)S(1)}, u32[]{:S(2)}, u32[]{:S(2)}) async-start(bf16[16,8,512]{2,1,0:T(8,128)(2,1)} %bitcast.25), calls=%async_computation.2 | async-start | bytes 262144 | tf_op jit(solution)/shard_map/all_to_all | solution.py:89
  82.6 1.6 fusion
  84.2 5.7 %all-to-all-done.2 = bf16[16,8,512]{2,1,0:T(8,128)(2,1)S(1)} async-done(((bf16[16,8,512]{2,1,0:T(8,128)(2,1)}), bf16[16,8,512]{2,1,0:T(8,128)(2,1)S(1)}, u32[]{:S(2)}, u32[]{:S(2)}) %all-to-all-start.2) | async-done | bytes 131104 | tf_op jit(solution)/shard_map/all_to_all | solution.py:89
  89.9 1.6 fusion.31
  92.1 2.4 fusion.9
  94.5 3.7 %all-to-all-start.3 = ((f32[16,8,512]{2,1,0:T(8,128)}), f32[16,8,512]{2,1,0:T(8,128)S(1)}, u32[]{:S(2)}, u32[]{:S(2)}) async-start(f32[16,8,512]{2,1,0:T(8,128)} %fusion.9), calls=%async_computation.3 | async-start | bytes 524288 | tf_op jit(solution)/shard_map/all_to_all | solution.py:93
  98.2 1.2 fusion.28
  99.4 2.3 convert_multiply_fusion.2
  101.7 2.9 copy.33
  104.6 2.8 all-to-all-done.3
  107.4 4.4 %scatter_custom_fusion = f32[1024,512]{1,0:T(8,128)} fusion(f32[1024,512]{1,0:T(8,128)} %copy.33, s32[128]{0:T(128)} %fusion.28, f32[16,8,512]{2,1,0:T(8,128)S(1)} %all-to-all-done.3), kind=kCustom, calls=%fused_computation.45 | custom fusion | flops 65536 | bytes 2359296 | tf_op jit(solution)/shard_map/scatter-add | solution.py:100
  111.7 2.9 copy.34
  114.8 4.3 %collective-permute-done.1 = f32[1024,512]{0,1:T(8,128)} collective-permute-done((f32[1024,512]{0,1:T(8,128)}, f32[1024,512]{0,1:T(8,128)}, u32[]{:S(2)}, u32[]{:S(2)}) %collective-permute-start.1) | collective-permute-done | bytes 2097184 | tf_op jit(solution)/shard_map/ppermute | solution.py:11
  119.1 2.6 multiply_reduce_fusion
  122.3 1.0 copy-done.9
  123.3 0.8 fusion.32
  124.0 1.4 copy-done.4
  125.4 8.2 %convolution_bitcast_fusion = f32[8,8,128,512]{2,3,1,0:T(8,128)} fusion(bf16[8,8,128,128]{3,2,1,0:T(8,128)(2,1)S(1)} %bitcast.109, f32[8,128,512]{2,1,0:T(8,128)S(1)} %bitcast.112, f32[8,128]{1,0:T(8,128)S(1)} %add_divide_fusion), kind=kOutput, calls=%fused_computation.8 | convolution fusion | flops 1074790400 | bytes 20975616 | tf_op jit(solution)/shard_map/ntij,niw->ntjw/dot_general | solution.py:23
  133.6 16.5 %copy.36 = f32[8,8,128,512]{3,2,1,0:T(8,128)} copy(f32[8,8,128,512]{2,3,1,0:T(8,128)} %convolution_bitcast_fusion) | data formatting | bytes 33554432 | tf_op jit(solution)/shard_map/ntij,niw->ntjw/dot_general | solution.py:23
  150.3 23.0 %scatter_fusion = f32[9,128,512]{2,1,0:T(8,128)S(1)} fusion(f32[9,128,512]{2,1,0:T(8,128)S(1)} %broadcast_in_dim.3, s32[64]{0:T(128)S(1)} %reshape.345, f32[64,128,512]{2,1,0:T(8,128)} %bitcast.106), kind=kCustom, calls=%fused_computation.6 | custom fusion | flops 4194304 | bytes 50331904 | tf_op jit(solution)/shard_map/scatter-add | solution.py:25
  173.4 3.2 slice_add_fusion
  177.3 3.9 %all-to-all-start.4 = ((bf16[16,8,512]{2,1,0:T(8,128)(2,1)}), bf16[16,8,512]{2,1,0:T(8,128)(2,1)S(1)}, u32[]{:S(2)}, u32[]{:S(2)}) async-start(bf16[16,8,512]{2,1,0:T(8,128)(2,1)} %fusion.19), calls=%async_computation.4 | async-start | bytes 262144 | tf_op jit(solution)/shard_map/all_to_all | solution.py:115
  181.2 3.3 fusion.33
  184.6 4.4 %all-to-all-done.4 = bf16[16,8,512]{2,1,0:T(8,128)(2,1)S(1)} async-done(((bf16[16,8,512]{2,1,0:T(8,128)(2,1)}), bf16[16,8,512]{2,1,0:T(8,128)(2,1)S(1)}, u32[]{:S(2)}, u32[]{:S(2)}) %all-to-all-start.4) | async-done | bytes 131104 | tf_op jit(solution)/shard_map/all_to_all | solution.py:115
  189.0 4.3 %scatter_custom_fusion.2 = f32[1024,512]{1,0:T(8,128)} fusion(f32[1024,512]{1,0:T(8,128)} %bitcast.118, s32[128]{0:T(128)S(1)} %fusion.29, bf16[16,8,512]{2,1,0:T(8,128)(2,1)S(1)} %all-to-all-done.4, f32[16,8]{1,0:T(8,128)S(1)} %copy-done.12), kind=kCustom, calls=%fused_computation.43 | custom fusion | flops 196608 | bytes 2236416 | tf_op jit(solution)/shard_map/scatter-add | solution.py:119
  193.3 3.9 %fusion.10 = f32[512,512]{1,0:T(8,128)} fusion(bf16[1024,512]{1,0:T(8,128)(2,1)S(1)} %bitcast.117, f32[1024,512]{1,0:T(8,128)} %scatter_custom_fusion.2, f32[1024,512]{1,0:T(8,128)} %get-tuple-element.24), kind=kOutput, calls=%fused_computation.37 | convolution fusion | flops 537919488 | bytes 6291456 | tf_op jit(solution)/shard_map/if,ih->fh/dot_general | solution.py:121
  198.5 131.0 %all-reduce.3.cloned.1.call-done = (f32[512,512]{1,0:T(8,128)}, f32[512,512]{1,0:T(8,128)}) async-done(((f32[512,512]{1,0:T(8,128)}, f32[512,512]{1,0:T(8,128)}), (f32[512,512]{1,0:T(8,128)}, f32[512,512]{1,0:T(8,128)})) %all-reduce.3.cloned.1.call-update) | async-done | bytes 2097168 | tf_op jit(solution)/shard_map/psum | solution.py:122
  329.5 2.4 copy.48
  331.9 1.0 copy.49
  (70 shorter events, 7.1 us)
Async XLA Ops:
  7.2 61.0 %copy-start = (bf16[512,512]{1,0:T(8,128)(2,1)S(1)}, bf16[512,512]{1,0:T(8,128)(2,1)}, u32[]{:S(2)}) copy-start(bf16[512,512]{1,0:T(8,128)(2,1)} %param.14) | copy-start | bytes 1572868
  7.2 16.7 %copy-start.19 = (s32[1,8,8]{2,1,0:T(8,128)S(1)}, s32[1,8,8]{2,1,0:T(8,128)}, u32[]{:S(2)}) copy-start(s32[1,8,8]{2,1,0:T(8,128)} %param.16) | copy-start | bytes 772
  7.2 16.8 %copy-start.2 = (bf16[1,64,128,128]{3,2,1,0:T(8,128)(2,1)S(1)}, bf16[1,64,128,128]{3,2,1,0:T(8,128)(2,1)}, u32[]{:S(2)}) copy-start(bf16[1,64,128,128]{3,2,1,0:T(8,128)(2,1)} %param.15) | copy-start | bytes 6291460
  15.5 16.1 %all-to-all-start = ((bf16[16,8,512]{2,1,0:T(8,128)(2,1)}), bf16[16,8,512]{2,1,0:T(8,128)(2,1)S(1)}, u32[]{:S(2)}, u32[]{:S(2)}) async-start(bf16[16,8,512]{2,1,0:T(8,128)(2,1)} %bitcast_multiply_fusion.1), calls=%async_computation | async-start | bytes 262144 | tf_op jit(solution)/shard_map/all_to_all | solution.py:69
  32.9 5.5 %copy-start.5 = (bf16[1024,512]{1,0:T(8,128)(2,1)S(1)}, bf16[1024,512]{1,0:T(8,128)(2,1)}, u32[]{:S(2)}) copy-start(bf16[1024,512]{1,0:T(8,128)(2,1)} %broadcast_multiply_fusion) | copy-start | bytes 3145732
  38.5 5.4 %copy-start.11 = (bf16[512,512]{1,0:T(8,128)(2,1)S(1)}, bf16[512,512]{1,0:T(8,128)(2,1)}, u32[]{:S(2)}) copy-start(bf16[512,512]{1,0:T(8,128)(2,1)} %param.13) | copy-start | bytes 1572868
  43.8 2.1 copy-start.6
  68.2 2.1 copy-start.8
  69.0 1.3 copy-start.16
  70.2 3.0 collective-permute-start
  78.4 11.5 %all-to-all-start.2 = ((bf16[16,8,512]{2,1,0:T(8,128)(2,1)}), bf16[16,8,512]{2,1,0:T(8,128)(2,1)S(1)}, u32[]{:S(2)}, u32[]{:S(2)}) async-start(bf16[16,8,512]{2,1,0:T(8,128)(2,1)} %bitcast.25), calls=%async_computation.2 | async-start | bytes 262144 | tf_op jit(solution)/shard_map/all_to_all | solution.py:89
  92.1 2.4 copy-start.14
  94.5 12.8 %all-to-all-start.3 = ((f32[16,8,512]{2,1,0:T(8,128)}), f32[16,8,512]{2,1,0:T(8,128)S(1)}, u32[]{:S(2)}, u32[]{:S(2)}) async-start(f32[16,8,512]{2,1,0:T(8,128)} %fusion.9), calls=%async_computation.3 | async-start | bytes 524288 | tf_op jit(solution)/shard_map/all_to_all | solution.py:93
  111.7 2.9 copy-start.17
  111.7 7.4 %copy-start.13 = (f32[1024]{0:T(1024)S(1)}, f32[1024]{0:T(1024)}, u32[]{:S(2)}) copy-start(f32[1024]{0:T(1024)} %get-tuple-element.18) | copy-start | bytes 12292
  111.7 7.4 %copy-start.15 = (f32[1024]{0:T(1024)S(1)}, f32[1024]{0:T(1024)}, u32[]{:S(2)}) copy-start(f32[1024]{0:T(1024)} %copy-done.14) | copy-start | bytes 12292
  114.6 4.5 %collective-permute-start.1 = (f32[1024,512]{0,1:T(8,128)}, f32[1024,512]{0,1:T(8,128)}, u32[]{:S(2)}, u32[]{:S(2)}) collective-permute-start(f32[1024,512]{0,1:T(8,128)} %copy.34), channel_id=1, source_target_pairs={{0,16},{16,0},{1,17},{17,1},{2,18},{18,2},{3,19},{19,3},{4,20},{20... | collective-permute-start | bytes 6291464 | tf_op jit(solution)/shard_map/ppermute | solution.py:11
  122.3 1.0 copy-start.9
  123.3 2.2 copy-start.3
  124.0 1.4 copy-start.4
  176.6 12.4 %copy-start.12 = (f32[16,8]{1,0:T(8,128)S(1)}, f32[16,8]{1,0:T(8,128)}, u32[]{:S(2)}) copy-start(f32[16,8]{1,0:T(8,128)} %get-tuple-element.21) | copy-start | bytes 1540
  177.3 11.7 %all-to-all-start.4 = ((bf16[16,8,512]{2,1,0:T(8,128)(2,1)}), bf16[16,8,512]{2,1,0:T(8,128)(2,1)S(1)}, u32[]{:S(2)}, u32[]{:S(2)}) async-start(bf16[16,8,512]{2,1,0:T(8,128)(2,1)} %fusion.19), calls=%async_computation.4 | async-start | bytes 262144 | tf_op jit(solution)/shard_map/all_to_all | solution.py:115
  181.2 12.1 %copy-start.7 = (bf16[8,128,512]{2,1,0:T(8,128)(2,1)S(1)}, bf16[8,128,512]{2,1,0:T(8,128)(2,1)}, u32[]{:S(2)}) copy-start(bf16[8,128,512]{2,1,0:T(8,128)(2,1)} %copy-done.6) | copy-start | bytes 3145732
  181.2 148.3 %all-reduce.3.cloned.1.call-start = ((), (), s32[]{:S(2)}) async-start(), calls=%async_computation.5 | async-start | bytes 4194304 | tf_op jit(solution)/shard_map/psum | solution.py:122
  197.2 0.7 copy-start.18
  329.5 2.4 copy-start.10
  329.5 3.4 copy-start.1
Sparse Core Ops, SparseCore 0:
  197.3 132.1 all-reduce.2
where the time goes:
time: 341 us; the launch traced here: 340 us
  waiting for transfers between devices  158 us (46%)
  other arithmetic  50.9 us (15%)
  local copies, waits for them, and re-layouts  50.3 us (15%)
  matrix products  36.3 us (11%)
  starting transfers between devices  19.5 us (6%)
  between operations  14.4 us (4%)
  blocking collectives  10.4 us (3%)
    psum x1, waiting for transfers between devices, per_device(): summed = lax.psum((grad_first, grad_second), ('view', 'dom'))  131 us
    scatter-add x1, other arithmetic, spread_back(): ext_grad = ext_grad.at[sources].add(spread)  23 us
    dot_general x1, local copies, waits for them, and re-layouts, spread_back(): jnp.einsum('ntij,niw->ntjw', tiles, scaled, preferred_element_type=jnp.fl...  16.5 us
    gather x2, local copies, waits for them, and re-layouts, mix_blocks(): picked = ext_blocks[sources]  11.1 us
    dot_general x2, matrix products, mix_blocks(): jnp.einsum('ntij,ntjw->niw', tiles, picked, preferred_element_type=jnp.fl...  10.7 us
    all_to_all x1, blocking collectives, per_device(): lax.all_to_all(hidden_out, 'dom', split_axis=0, concat_axis=0, tiled=True)  10.4 us
    all_to_all x1, starting transfers between devices, per_device(): lax.all_to_all(outgoing, 'dom', split_axis=0, concat_axis=0, tiled=True)  8.34 us
    dot_general x1, matrix products, spread_back(): jnp.einsum('ntij,niw->ntjw', tiles, scaled, preferred_element_type=jnp.fl...  8.17 us
  transfers between devices with their start and end apart: 7, of which 7 were waited for; matrix products, arithmetic and copies ran while one was open for 4% of the time, Pallas kernels for 0%

commit v1 on v0

--- a/solution.py
+++ b/solution.py
@@ -119,7 +119,7 @@
     g_hidden = flat_grad[:row_count].at[send_rows.reshape(-1)].add(back_grad.reshape(-1, hid_width))
     g_pre = jnp.where(pre_act > 0, g_hidden, 0.0).astype(jnp.bfloat16)
     grad_first = jnp.einsum("if,ih->fh", mixed_first, g_pre, preferred_element_type=jnp.float32)
-    summed = lax.psum((grad_first, grad_second), ("view", "dom"))
+    summed = lax.psum(lax.psum((grad_first, grad_second), "dom"), "view")
     return (node_loss[None, :], summed[0], summed[1])
 
 

time: 341 us -> 356 us (1.044)
  waiting for transfers between devices: 158 us -> 174 us
    psum x1 -> x2, waiting for transfers between devices: 131 us -> 147 us  [per_device(): summed = lax.psum(lax.psum((grad_first, grad_second), 'dom'), 'view')]
  transfers between devices with their start and end apart: 7 -> 8, of which waited for: 7 -> 8; matrix products, arithmetic and copies ran while one was open for 4% -> 4% of each run, Pallas kernels for 0% -> 0%
where the time goes in v1:
time: 356 us; the launch traced here: 355 us
  waiting for transfers between devices  174 us (49%)
  other arithmetic  50.9 us (14%)
  local copies, waits for them, and re-layouts  49.6 us (14%)
  matrix products  36.3 us (10%)
  starting transfers between devices  19.6 us (6%)
  between operations  14.4 us (4%)
  blocking collectives  10.4 us (3%)
    psum x2, waiting for transfers between devices, per_device(): summed = lax.psum(lax.psum((grad_first, grad_second), 'dom'), 'view')  147 us
    scatter-add x1, other arithmetic, spread_back(): ext_grad = ext_grad.at[sources].add(spread)  23 us
    dot_general x1, local copies, waits for them, and re-layouts, spread_back(): jnp.einsum('ntij,niw->ntjw', tiles, scaled, preferred_element_type=jnp.fl...  16.5 us
    gather x2, local copies, waits for them, and re-layouts, mix_blocks(): picked = ext_blocks[sources]  11 us
    dot_general x2, matrix products, mix_blocks(): jnp.einsum('ntij,ntjw->niw', tiles, picked, preferred_element_type=jnp.fl...  10.6 us
    all_to_all x1, blocking collectives, per_device(): lax.all_to_all(hidden_out, 'dom', split_axis=0, concat_axis=0, tiled=True)  10.4 us
    all_to_all x1, starting transfers between devices, per_device(): lax.all_to_all(outgoing, 'dom', split_axis=0, concat_axis=0, tiled=True)  8.34 us
    dot_general x1, matrix products, spread_back(): jnp.einsum('ntij,niw->ntjw', tiles, scaled, preferred_element_type=jnp.fl...  8.19 us
  transfers between devices with their start and end apart: 8, of which 8 were waited for; matrix products, arithmetic and copies ran while one was open for 4% of the time, Pallas kernels for 0%

profile of v1, /device:TPU:0, one launch (start us, length us, event | category | flops | bytes accessed | tf_op | source)
XLA Modules:
  0.0 354.8 jit_solution(3851825764110285840)
XLA Ops:
  7.2 0.9 convert_reduce_fusion.1
  8.9 1.3 fusion.26
  10.2 2.3 broadcast_multiply_fusion
  12.5 2.2 gather_fusion
  15.5 8.3 %all-to-all-start = ((bf16[16,8,512]{2,1,0:T(8,128)(2,1)}), bf16[16,8,512]{2,1,0:T(8,128)(2,1)S(1)}, u32[]{:S(2)}, u32[]{:S(2)}) async-start(bf16[16,8,512]{2,1,0:T(8,128)(2,1)} %bitcast_multiply_fusion.1), calls=%async_computation | async-start | bytes 262144 | tf_op jit(solution)/shard_map/all_to_all | solution.py:69
  24.6 7.0 %all-to-all-done = bf16[16,8,512]{2,1,0:T(8,128)(2,1)S(1)} async-done(((bf16[16,8,512]{2,1,0:T(8,128)(2,1)}), bf16[16,8,512]{2,1,0:T(8,128)(2,1)S(1)}, u32[]{:S(2)}, u32[]{:S(2)}) %all-to-all-start) | async-done | bytes 131104 | tf_op jit(solution)/shard_map/all_to_all | solution.py:69
  31.6 1.3 pad_maximum_fusion
  33.0 5.5 %gather_fusion.1 = bf16[64,128,512]{2,1,0:T(8,128)(2,1)} fusion(bf16[9,128,512]{2,1,0:T(8,128)(2,1)S(1)} %bitcast.105, s32[1024]{0:T(1024)S(1)} %pad_clamp_fusion.1), kind=kCustom, calls=%fused_computation.1 | custom fusion | bytes 16777472 | tf_op jit(solution)/shard_map/gather | solution.py:15
  38.5 5.3 %fusion.7 = bf16[8,128,512]{2,1,0:T(8,128)(2,1)S(1)} fusion(bf16[8,128,512]{2,1,0:T(8,128)(2,1)S(1)} %bitcast.114, bf16[8,8,128,128]{3,2,1,0:T(8,128)(2,1)} %bitcast.107, bf16[8,8,128,512]{3,2,1,0:T(8,128)(2,1)} %bitcast.111, f32[8,128]{1,0:T(8,128)S(1)} %add_divide_fusion), kind=kOutput, calls=%fused_computation.23 | convolution fusion | flops 1075838976 | bytes 12587008 | tf_op jit(solution)/shard_map/ntij,ntjw->niw/dot_general | solution.py:16
  43.8 2.0 maximum_convert_fusion
  45.9 0.8 gather_fusion.2
  46.8 10.4 %all_to_all.25 = bf16[16,8,512]{2,1,0:T(8,128)(2,1)S(1)} all-to-all(bf16[16,8,512]{2,1,0:T(8,128)(2,1)S(1)} %bitcast_multiply_fusion), channel_id=1, replica_groups=mesh['view'=2,'dom'=16] {'dom'}, dimensions={0} | all-to-all | bytes 262144 | tf_op jit(solution)/shard_map/all_to_all | solution.py:77
  57.3 5.5 %gather_fusion.3 = bf16[64,128,512]{2,1,0:T(8,128)(2,1)} fusion(bf16[9,128,512]{2,1,0:T(8,128)(2,1)S(1)} %bitcast.104, s32[1024]{0:T(1024)S(1)} %pad_clamp_fusion.1), kind=kCustom, calls=%fused_computation.3 | custom fusion | bytes 16777472 | tf_op jit(solution)/shard_map/gather | solution.py:15
  62.8 5.3 %fusion.5 = bf16[8,128,512]{2,1,0:T(8,128)(2,1)S(1)} fusion(bf16[8,128,512]{2,1,0:T(8,128)(2,1)S(1)} %bitcast.115, bf16[8,8,128,128]{3,2,1,0:T(8,128)(2,1)} %bitcast.108, bf16[8,8,128,512]{3,2,1,0:T(8,128)(2,1)} %bitcast.110, f32[8,128]{1,0:T(8,128)S(1)} %add_divide_fusion), kind=kOutput, calls=%fused_computation.20 | convolution fusion | flops 1075838976 | bytes 12587008 | tf_op jit(solution)/shard_map/ntij,ntjw->niw/dot_general | solution.py:16
  68.1 0.8 multiply_reduce_fusion.1
  69.0 1.2 multiply_convert_fusion.2
  70.4 2.8 collective-permute-done
  73.2 2.3 copy.31
  75.5 2.9 gather_fusion.4
  78.4 3.5 all-to-all-start.2
  82.6 1.6 fusion
  84.2 5.7 %all-to-all-done.2 = bf16[16,8,512]{2,1,0:T(8,128)(2,1)S(1)} async-done(((bf16[16,8,512]{2,1,0:T(8,128)(2,1)}), bf16[16,8,512]{2,1,0:T(8,128)(2,1)S(1)}, u32[]{:S(2)}, u32[]{:S(2)}) %all-to-all-start.2) | async-done | bytes 131104 | tf_op jit(solution)/shard_map/all_to_all | solution.py:89
  89.9 1.6 fusion.31
  92.0 2.4 fusion.9
  94.5 3.7 %all-to-all-start.3 = ((f32[16,8,512]{2,1,0:T(8,128)}), f32[16,8,512]{2,1,0:T(8,128)S(1)}, u32[]{:S(2)}, u32[]{:S(2)}) async-start(f32[16,8,512]{2,1,0:T(8,128)} %fusion.9), calls=%async_computation.3 | async-start | bytes 524288 | tf_op jit(solution)/shard_map/all_to_all | solution.py:93
  98.2 1.2 fusion.28
  99.4 2.3 convert_multiply_fusion.2
  101.6 2.9 copy.33
  104.6 2.7 all-to-all-done.3
  107.3 4.3 %scatter_custom_fusion = f32[1024,512]{1,0:T(8,128)} fusion(f32[1024,512]{1,0:T(8,128)} %copy.33, s32[128]{0:T(128)} %fusion.28, f32[16,8,512]{2,1,0:T(8,128)S(1)} %all-to-all-done.3), kind=kCustom, calls=%fused_computation.45 | custom fusion | flops 65536 | bytes 2359296 | tf_op jit(solution)/shard_map/scatter-add | solution.py:100
  111.7 2.9 copy.34
  114.8 4.3 %collective-permute-done.1 = f32[1024,512]{0,1:T(8,128)} collective-permute-done((f32[1024,512]{0,1:T(8,128)}, f32[1024,512]{0,1:T(8,128)}, u32[]{:S(2)}, u32[]{:S(2)}) %collective-permute-start.1) | collective-permute-done | bytes 2097184 | tf_op jit(solution)/shard_map/ppermute | solution.py:11
  119.1 2.6 multiply_reduce_fusion
  122.3 1.0 copy-done.9
  124.0 1.4 copy-done.4
  125.4 8.2 %convolution_bitcast_fusion = f32[8,8,128,512]{2,3,1,0:T(8,128)} fusion(bf16[8,8,128,128]{3,2,1,0:T(8,128)(2,1)S(1)} %bitcast.109, f32[8,128,512]{2,1,0:T(8,128)S(1)} %bitcast.112, f32[8,128]{1,0:T(8,128)S(1)} %add_divide_fusion), kind=kOutput, calls=%fused_computation.8 | convolution fusion | flops 1074790400 | bytes 20975616 | tf_op jit(solution)/shard_map/ntij,niw->ntjw/dot_general | solution.py:23
  133.6 16.5 %copy.36 = f32[8,8,128,512]{3,2,1,0:T(8,128)} copy(f32[8,8,128,512]{2,3,1,0:T(8,128)} %convolution_bitcast_fusion) | data formatting | bytes 33554432 | tf_op jit(solution)/shard_map/ntij,niw->ntjw/dot_general | solution.py:23
  150.3 23.0 %scatter_fusion = f32[9,128,512]{2,1,0:T(8,128)S(1)} fusion(f32[9,128,512]{2,1,0:T(8,128)S(1)} %broadcast_in_dim.3, s32[64]{0:T(128)S(1)} %reshape.345, f32[64,128,512]{2,1,0:T(8,128)} %bitcast.106), kind=kCustom, calls=%fused_computation.6 | custom fusion | flops 4194304 | bytes 50331904 | tf_op jit(solution)/shard_map/scatter-add | solution.py:25
  173.4 3.2 slice_add_fusion
  177.2 3.9 %all-to-all-start.4 = ((bf16[16,8,512]{2,1,0:T(8,128)(2,1)}), bf16[16,8,512]{2,1,0:T(8,128)(2,1)S(1)}, u32[]{:S(2)}, u32[]{:S(2)}) async-start(bf16[16,8,512]{2,1,0:T(8,128)(2,1)} %fusion.19), calls=%async_computation.4 | async-start | bytes 262144 | tf_op jit(solution)/shard_map/all_to_all | solution.py:115
  181.2 3.3 fusion.33
  184.5 4.4 %all-to-all-done.4 = bf16[16,8,512]{2,1,0:T(8,128)(2,1)S(1)} async-done(((bf16[16,8,512]{2,1,0:T(8,128)(2,1)}), bf16[16,8,512]{2,1,0:T(8,128)(2,1)S(1)}, u32[]{:S(2)}, u32[]{:S(2)}) %all-to-all-start.4) | async-done | bytes 131104 | tf_op jit(solution)/shard_map/all_to_all | solution.py:115
  188.9 4.3 %scatter_custom_fusion.2 = f32[1024,512]{1,0:T(8,128)} fusion(f32[1024,512]{1,0:T(8,128)} %bitcast.118, s32[128]{0:T(128)S(1)} %fusion.29, bf16[16,8,512]{2,1,0:T(8,128)(2,1)S(1)} %all-to-all-done.4, f32[16,8]{1,0:T(8,128)S(1)} %copy-done.12), kind=kCustom, calls=%fused_computation.43 | custom fusion | flops 196608 | bytes 2236416 | tf_op jit(solution)/shard_map/scatter-add | solution.py:119
  193.2 3.9 %fusion.10 = f32[512,512]{1,0:T(8,128)} fusion(bf16[1024,512]{1,0:T(8,128)(2,1)S(1)} %bitcast.117, f32[1024,512]{1,0:T(8,128)} %scatter_custom_fusion.2, f32[1024,512]{1,0:T(8,128)} %get-tuple-element.26), kind=kOutput, calls=%fused_computation.37 | convolution fusion | flops 537919488 | bytes 6291456 | tf_op jit(solution)/shard_map/if,ih->fh/dot_general | solution.py:121
  197.2 124.4 %all-reduce.5.cloned.1.call-done = (f32[512,512]{1,0:T(8,128)}, f32[512,512]{1,0:T(8,128)}) async-done(((f32[512,512]{1,0:T(8,128)}, f32[512,512]{1,0:T(8,128)}), (f32[512,512]{1,0:T(8,128)}, f32[512,512]{1,0:T(8,128)})) %all-reduce.5.cloned.1.call-update) | async-done | bytes 2097168 | tf_op jit(solution)/shard_map/psum | solution.py:122
  322.3 22.4 %all-reduce.7.cloned.1.call-done = (f32[512,512]{1,0:T(8,128)}, f32[512,512]{1,0:T(8,128)}) async-done(((f32[512,512]{1,0:T(8,128)}, f32[512,512]{1,0:T(8,128)}), (f32[512,512]{1,0:T(8,128)}, f32[512,512]{1,0:T(8,128)})) %all-reduce.7.cloned.1.call-update) | async-done | bytes 2097168 | tf_op jit(solution)/shard_map/psum | solution.py:122
  344.6 2.4 copy.50
  347.0 1.0 copy.51
  (73 shorter events, 7.2 us)
Async XLA Ops:
  7.2 61.0 %copy-start = (bf16[512,512]{1,0:T(8,128)(2,1)S(1)}, bf16[512,512]{1,0:T(8,128)(2,1)}, u32[]{:S(2)}) copy-start(bf16[512,512]{1,0:T(8,128)(2,1)} %param.14) | copy-start | bytes 1572868
  7.2 16.7 %copy-start.19 = (s32[1,8,8]{2,1,0:T(8,128)S(1)}, s32[1,8,8]{2,1,0:T(8,128)}, u32[]{:S(2)}) copy-start(s32[1,8,8]{2,1,0:T(8,128)} %param.16) | copy-start | bytes 772
  7.2 16.8 %copy-start.2 = (bf16[1,64,128,128]{3,2,1,0:T(8,128)(2,1)S(1)}, bf16[1,64,128,128]{3,2,1,0:T(8,128)(2,1)}, u32[]{:S(2)}) copy-start(bf16[1,64,128,128]{3,2,1,0:T(8,128)(2,1)} %param.15) | copy-start | bytes 6291460
  15.5 16.1 %all-to-all-start = ((bf16[16,8,512]{2,1,0:T(8,128)(2,1)}), bf16[16,8,512]{2,1,0:T(8,128)(2,1)S(1)}, u32[]{:S(2)}, u32[]{:S(2)}) async-start(bf16[16,8,512]{2,1,0:T(8,128)(2,1)} %bitcast_multiply_fusion.1), calls=%async_computation | async-start | bytes 262144 | tf_op jit(solution)/shard_map/all_to_all | solution.py:69
  32.9 5.5 %copy-start.5 = (bf16[1024,512]{1,0:T(8,128)(2,1)S(1)}, bf16[1024,512]{1,0:T(8,128)(2,1)}, u32[]{:S(2)}) copy-start(bf16[1024,512]{1,0:T(8,128)(2,1)} %broadcast_multiply_fusion) | copy-start | bytes 3145732
  38.5 5.4 %copy-start.11 = (bf16[512,512]{1,0:T(8,128)(2,1)S(1)}, bf16[512,512]{1,0:T(8,128)(2,1)}, u32[]{:S(2)}) copy-start(bf16[512,512]{1,0:T(8,128)(2,1)} %param.13) | copy-start | bytes 1572868
  43.8 2.1 copy-start.6
  68.1 2.1 copy-start.8
  68.9 1.3 copy-start.16
  70.2 3.0 collective-permute-start
  78.4 11.5 %all-to-all-start.2 = ((bf16[16,8,512]{2,1,0:T(8,128)(2,1)}), bf16[16,8,512]{2,1,0:T(8,128)(2,1)S(1)}, u32[]{:S(2)}, u32[]{:S(2)}) async-start(bf16[16,8,512]{2,1,0:T(8,128)(2,1)} %bitcast.25), calls=%async_computation.2 | async-start | bytes 262144 | tf_op jit(solution)/shard_map/all_to_all | solution.py:89
  92.0 2.4 copy-start.14
  94.5 12.8 %all-to-all-start.3 = ((f32[16,8,512]{2,1,0:T(8,128)}), f32[16,8,512]{2,1,0:T(8,128)S(1)}, u32[]{:S(2)}, u32[]{:S(2)}) async-start(f32[16,8,512]{2,1,0:T(8,128)} %fusion.9), calls=%async_computation.3 | async-start | bytes 524288 | tf_op jit(solution)/shard_map/all_to_all | solution.py:93
  111.7 2.9 copy-start.17
  111.7 7.4 %copy-start.13 = (f32[1024]{0:T(1024)S(1)}, f32[1024]{0:T(1024)}, u32[]{:S(2)}) copy-start(f32[1024]{0:T(1024)} %get-tuple-element.20) | copy-start | bytes 12292
  111.7 7.4 %copy-start.15 = (f32[1024]{0:T(1024)S(1)}, f32[1024]{0:T(1024)}, u32[]{:S(2)}) copy-start(f32[1024]{0:T(1024)} %copy-done.14) | copy-start | bytes 12292
  114.6 4.5 %collective-permute-start.1 = (f32[1024,512]{0,1:T(8,128)}, f32[1024,512]{0,1:T(8,128)}, u32[]{:S(2)}, u32[]{:S(2)}) collective-permute-start(f32[1024,512]{0,1:T(8,128)} %copy.34), channel_id=1, source_target_pairs={{0,16},{16,0},{1,17},{17,1},{2,18},{18,2},{3,19},{19,3},{4,20},{20... | collective-permute-start | bytes 6291464 | tf_op jit(solution)/shard_map/ppermute | solution.py:11
  122.2 1.0 copy-start.9
  123.2 2.2 copy-start.3
  124.0 1.4 copy-start.4
  176.6 12.4 %copy-start.12 = (f32[16,8]{1,0:T(8,128)S(1)}, f32[16,8]{1,0:T(8,128)}, u32[]{:S(2)}) copy-start(f32[16,8]{1,0:T(8,128)} %get-tuple-element.23) | copy-start | bytes 1540
  177.2 11.7 %all-to-all-start.4 = ((bf16[16,8,512]{2,1,0:T(8,128)(2,1)}), bf16[16,8,512]{2,1,0:T(8,128)(2,1)S(1)}, u32[]{:S(2)}, u32[]{:S(2)}) async-start(bf16[16,8,512]{2,1,0:T(8,128)(2,1)} %fusion.19), calls=%async_computation.4 | async-start | bytes 262144 | tf_op jit(solution)/shard_map/all_to_all | solution.py:115
  181.1 12.1 %copy-start.7 = (bf16[8,128,512]{2,1,0:T(8,128)(2,1)S(1)}, bf16[8,128,512]{2,1,0:T(8,128)(2,1)}, u32[]{:S(2)}) copy-start(bf16[8,128,512]{2,1,0:T(8,128)(2,1)} %copy-done.6) | copy-start | bytes 3145732
  181.1 140.5 %all-reduce.5.cloned.1.call-start = ((), (), s32[]{:S(2)}) async-start(), calls=%async_computation.5 | async-start | bytes 4194304 | tf_op jit(solution)/shard_map/psum | solution.py:122
  197.2 124.5 %copy-start.18 = (f32[1024]{0:T(1024)S(1)}, f32[1024]{0:T(1024)}, u32[]{:S(2)}) copy-start(f32[1024]{0:T(1024)} %get-tuple-element.22) | copy-start | bytes 12292
  197.2 147.5 %all-reduce.7.cloned.1.call-start = ((), (), s32[]{:S(2)}) async-start(), calls=%async_computation.6 | async-start | bytes 4194304 | tf_op jit(solution)/shard_map/psum | solution.py:122
  344.6 2.4 copy-start.10
  344.6 3.4 copy-start.1
Sparse Core Ops, SparseCore 0:
  197.3 124.2 all-reduce.4
  324.0 20.5 all-reduce.6
